TPU v7x, 32 devices: a whole 2x2x4 slice. The times are simulated.
32 devices in a mesh: groups: 2 (over y), seq: 4 (over z), mp: 2 (over x), section: 2 (over core).
Axes of the slice: x: 2, y: 2, z: 4, core: 2. Of those that a mesh axis runs over, the one named last changes fastest.
Arguments:
- features: bfloat16 [4, 512, 8192], P(('groups', 'section'), 'mp', 'seq'), parts along dimension 0, may hold values from -6 to 6
- alpha: float32 [512], P('mp'), may hold values from 0.5 to 2
- conv_weight: bfloat16 [1024, 32, 16], P('mp'), may hold values from -0.25 to 0.25
- qkv_weight: bfloat16 [1024, 3, 1024], P(None, None, 'mp'), may hold values from -1 to 1
- readout: float32 [1024], P('mp'), may hold values from -4 to 4
- offsets: int32 [4], P(('groups', 'section')), parts along dimension 0, may hold values from 0 to 14479
- pairs: int32 [8, 2], P('groups'), parts along dimension 0, may hold values from 0 to 1
- labels: int32 [8], P('groups'), parts along dimension 0, may hold values from 0 to 1
Outputs:
- grads: bfloat16 [3, 4, 1024, 1024], P(None, ('groups', 'section'), 'seq', 'mp'), parts along dimension 1
- rewards: float32 [4], P('groups'), parts along dimension 0
- loss: float32 [2], P('groups'), parts along dimension 0
There are 2 independent parts, one for each index of `groups`. A program takes and returns all parts, laid end to end along the dimension named above; an argument that names none is the same for every part. Nothing has to cross between parts.
All inputs are finite; a program needn't handle non-finite values.
Results may differ from a plain program's by a relative error of at most 0.017.
Values may be sent and summed in bfloat16 or wider, within the bound.
A program may use at most 64 MiB of HBM per device.

v0:
```python
import math
import jax
import jax.numpy as jnp
from jax import lax
from jax.sharding import PartitionSpec as P

D = 1024
HD = 64
EPS = 1e-06
BASE = 10000.0


def padded_2(block, sides, width):
    for axis, dim in sides:
        count = lax.axis_size(axis)
        forward = [(i, i + 1) for i in range(count - 1)]
        backward = [(target, source) for source, target in forward]
        low = lax.ppermute(
            lax.slice_in_dim(block, block.shape[dim] - width, None, axis=dim), axis, forward
        )
        high = lax.ppermute(lax.slice_in_dim(block, 0, width, axis=dim), axis, backward)
        block = jnp.concatenate([low, block, high], axis=dim)
    return block


def position_table(positions, feature_ids, width):
    pair_ids = (feature_ids // 2).astype(jnp.float32)
    freqs = jnp.exp(pair_ids * (-2.0 * math.log(BASE) / width))
    angle = positions.astype(jnp.float32)[..., None] * freqs
    return jnp.where(feature_ids % 2 == 0, jnp.sin(angle), jnp.cos(angle))


def local(features, alpha, conv_weight, qkv_weight, readout, offsets, pairs, labels):
    f32 = jnp.float32
    bf16 = jnp.bfloat16
    cand, chans, samples = features.shape
    local_width = conv_weight.shape[0]
    per_group = conv_weight.shape[1]
    kern = conv_weight.shape[2]
    stride = kern // 2
    frames_dev = samples // stride
    groups_here = chans // per_group
    heads_here = local_width // HD
    raw = features.astype(f32)
    slope = alpha[None, :, None]
    act = (raw + jnp.sin(slope * raw) ** 2 / slope).astype(bf16)
    padded = padded_2(act, (("seq", 2),), stride // 2)
    blocks = padded.reshape(cand, groups_here, per_group, frames_dev + 1, stride).transpose(
        0, 1, 3, 2, 4
    )
    patches = jnp.concatenate([blocks[:, :, :-1], blocks[:, :, 1:]], axis=-1).reshape(
        cand, groups_here, frames_dev, per_group * kern
    )
    kernel = conv_weight.reshape(groups_here, local_width // groups_here, per_group * kern)
    frames = jnp.einsum("cgfk,gok->cfgo", patches, kernel, preferred_element_type=f32).reshape(
        cand, frames_dev, local_width
    )
    slice_id = lax.axis_index("seq")
    part_id = lax.axis_index("mp")
    positions = (
        offsets[:, None] + slice_id * frames_dev + jnp.arange(frames_dev, dtype=jnp.int32)[None, :]
    )
    feature_ids = part_id * local_width + jnp.arange(local_width, dtype=jnp.int32)
    resid = (frames + position_table(positions, feature_ids, D)).astype(bf16)
    whole = lax.all_gather(resid, "mp", axis=2, tiled=True)
    squares = jnp.mean(jnp.square(whole.astype(f32)), axis=-1)
    projected = jnp.einsum("cfd,dtk->cftk", whole, qkv_weight, preferred_element_type=f32)
    qkv = (projected * lax.rsqrt(squares + EPS)[:, :, None, None]).astype(bf16)
    query = qkv[:, :, 0]
    keys, values = (
        lax.all_gather(qkv[:, :, 1], "seq", axis=1, tiled=True),
        lax.all_gather(qkv[:, :, 2], "seq", axis=1, tiled=True),
    )
    total = keys.shape[1]
    block = min(512, total)
    count_blocks = total // block
    scale = 1.0 / math.sqrt(HD)
    query4 = query.reshape(cand, frames_dev, heads_here, HD)

    def key_slice(source, start, size):
        return lax.dynamic_slice_in_dim(source, start, size, 1).reshape(cand, size, heads_here, HD)

    def scores_for(start, size):
        return (
            jnp.einsum(
                "cfhe,ckhe->chfk", query4, key_slice(keys, start, size), preferred_element_type=f32
            )
            * scale
        )

    def stat_step(carry, index):
        peak_now, mass_now = carry
        score = scores_for(index * block, block)
        fresh = jnp.maximum(peak_now, jnp.max(score, axis=-1))
        mass_now = mass_now * jnp.exp(peak_now - fresh) + jnp.sum(
            jnp.exp(score - fresh[..., None]), axis=-1
        )
        return ((fresh, mass_now), None)

    start_peak = jnp.full((cand, heads_here, frames_dev), -jnp.inf, f32)
    (peak, mass), _ = lax.scan(
        stat_step, (start_peak, jnp.zeros_like(start_peak)), jnp.arange(count_blocks)
    )

    def weights_for(start, size):
        return jnp.exp(scores_for(start, size) - peak[..., None]) / mass[..., None]

    def out_step(running, index):
        start = index * block
        prob = weights_for(start, block).astype(bf16)
        running = running + jnp.einsum(
            "chfk,ckhe->cfhe", prob, key_slice(values, start, block), preferred_element_type=f32
        )
        return (running, None)

    attended4, _ = lax.scan(
        out_step, jnp.zeros((cand, frames_dev, heads_here, HD), f32), jnp.arange(count_blocks)
    )
    attended = attended4.reshape(cand, frames_dev, local_width)
    gate = jax.nn.sigmoid(lax.optimization_barrier(resid).astype(f32))
    section_id = lax.axis_index("section")
    all_cands = cand * lax.axis_size("section")
    owner = (
        jnp.arange(all_cands, dtype=jnp.int32)[None, :]
        == (section_id * cand + jnp.arange(cand, dtype=jnp.int32))[:, None]
    ).astype(f32)
    partial_rewards = jnp.sum(attended * gate * readout, axis=(1, 2)) / math.sqrt(total)
    rewards = lax.psum(jnp.sum(owner * partial_rewards[:, None], axis=0), ("seq", "mp", "section"))
    chosen = (pairs[:, :, None] == jnp.arange(all_cands, dtype=jnp.int32)[None, None, :]).astype(
        f32
    )
    paired = jnp.sum(chosen * rewards[None, None, :], axis=-1)
    margin = paired[:, 0] - paired[:, 1]
    target = labels.astype(f32)
    loss = jnp.sum(jax.nn.softplus(margin) - target * margin)
    coeff = jax.nn.sigmoid(margin) - target
    reward_grad = jnp.sum(coeff[:, None] * (chosen[:, 0] - chosen[:, 1]), axis=0)
    own_grad = jnp.sum(owner * reward_grad[None, :], axis=1)
    upstream = (own_grad[:, None, None] * readout * gate).astype(bf16)
    upstream4 = upstream.reshape(cand, frames_dev, heads_here, HD)
    delta = jnp.sum(upstream4.astype(f32) * attended4, axis=-1).transpose(0, 2, 1)

    def backward_block(start, size):
        prob = weights_for(start, size)
        prob_low = prob.astype(bf16)
        dprob = jnp.einsum(
            "cfhe,ckhe->chfk", upstream4, key_slice(values, start, size), preferred_element_type=f32
        )
        dscore = (prob * (dprob - delta[..., None])).astype(bf16)
        dquery = (
            jnp.einsum(
                "chfk,ckhe->cfhe", dscore, key_slice(keys, start, size), preferred_element_type=f32
            )
            * scale
        )
        dkey = jnp.einsum("chfk,cfhe->kche", dscore, query4, preferred_element_type=f32) * scale
        dvalue = jnp.einsum("chfk,cfhe->kche", prob_low, upstream4, preferred_element_type=f32)
        term = jnp.concatenate(
            [dkey.reshape(size, cand, local_width), dvalue.reshape(size, cand, local_width)],
            axis=-1,
        )
        return (dquery, term)

    zero_query = jnp.zeros((cand, frames_dev, heads_here, HD), f32)

    def grad_step(running, index):
        dquery, term = backward_block(index * block, block)
        return (running + dquery, term.astype(bf16))

    grad_query, stored = lax.scan(grad_step, zero_query, jnp.arange(count_blocks))
    stacked = stored.reshape(total, cand, 2 * local_width)
    summed = lax.psum_scatter(
        stacked.astype(f32).astype(jnp.bfloat16), "seq", scatter_dimension=0, tiled=True
    ).astype(jnp.float32)
    grad_key = summed[:, :, :local_width].transpose(1, 0, 2)
    grad_value = summed[:, :, local_width:].transpose(1, 0, 2)
    grads = jnp.stack(
        [grad_query.reshape(cand, frames_dev, local_width), grad_key, grad_value], axis=0
    ).astype(bf16)
    return (grads, rewards, loss.reshape(1))


def solution(mesh):
    placed = (
        P(("groups", "section"), "mp", "seq"),
        P("mp"),
        P("mp", None, None),
        P(None, None, "mp"),
        P("mp"),
        P(("groups", "section")),
        P("groups", None),
        P("groups"),
    )
    return jax.shard_map(
        local,
        mesh=mesh,
        in_specs=placed,
        out_specs=(P(None, ("groups", "section"), "seq", "mp"), P("groups"), P("groups")),
        check_vma=False,
    )
```

profile of v0, /device:TPU:0, one launch (start us, length us, event | category | flops | bytes accessed | tf_op | source)
XLA Modules:
  0.0 278.7 jit_solution(6267920341593110061)
XLA Ops:
  7.2 8.6 %fusion.25 = bf16[1,256,2048]{2,1,0:T(8,128)(2,1)S(1)} fusion(bf16[1,256,2048]{2,1,0:T(8,128)(2,1)} %param.14, f32[256]{0:T(256)} %param.15), kind=kLoop, calls=%fused_computation.40 | loop fusion | flops 3145728 | bytes 2098176 | tf_op jit(solution)/shard_map/convert_element_type | solution.py:46
  17.0 4.9 %collective-permute-start = (bf16[1,256,4]{2,1,0:T(8,128)(2,1)S(1)}, bf16[1,256,4]{2,1,0:T(8,128)(2,1)S(1)}, u32[]{:S(2)}, u32[]{:S(2)}) collective-permute-start(bf16[1,256,4]{2,1,0:T(8,128)(2,1)S(1)} %get-tuple-element.365), channel_id=1, source_target_pairs={{0,4},{4,8},{8,12},{1,5},{5,9},{9,13},{2,6},{6,10},{10,14},{3,7},{... | collective-permute-start | bytes 6152 | tf_op jit(solution)/shard_map/ppermute | solution.py:18
  24.1 2.4 reshape.438
  28.1 3.5 %concatenate.32 = bf16[1,256,2056]{2,1,0:T(8,128)(2,1)} concatenate(bf16[1,256,4]{2,1,0:T(8,128)(2,1)S(1)} %collective-permute-done, bf16[1,256,2048]{2,1,0:T(8,128)(2,1)} %copy-done.5, bf16[1,256,4]{2,1,0:T(8,128)(2,1)S(1)} %collective-permute-done.1), dimensions={2} | concatenate | bytes 2105344 | tf_op jit(solution)/shard_map/concatenate | solution.py:22
  31.6 2.3 copy.41
  33.9 5.8 %reshape.436 = bf16[1,8,32,257,8]{2,1,4,3,0:T(8,128)(2,1)} reshape(bf16[1,256,2056]{1,2,0:T(8,128)(2,1)} %copy.41) | data formatting | bytes 2105344 | tf_op jit(solution)/shard_map/reshape | solution.py:48
  39.7 6.5 %fusion.53 = (bf16[1,8,256,32,8]{3,1,4,2,0:T(8,128)(2,1)}, bf16[1,8,256,32,8]{3,1,4,2,0:T(8,128)(2,1)}) fusion(bf16[1,8,257,32,8]{3,1,4,2,0:T(8,128)(2,1)} %bitcast.233), kind=kLoop, calls=%fused_computation.102 | loop fusion | bytes 4194304 | tf_op jit(solution)/shard_map/slice | solution.py:51
  46.2 7.7 %copy.42 = bf16[1,8,256,32,8]{2,4,3,1,0:T(8,128)(2,1)} copy(bf16[1,8,256,32,8]{3,1,4,2,0:T(8,128)(2,1)} %get-tuple-element.362) | data formatting | bytes 2097152 | tf_op jit(solution)/shard_map/slice | solution.py:51
  53.9 7.7 %copy.43 = bf16[1,8,256,32,8]{2,4,3,1,0:T(8,128)(2,1)} copy(bf16[1,8,256,32,8]{3,1,4,2,0:T(8,128)(2,1)} %get-tuple-element.363) | data formatting | bytes 2097152 | tf_op jit(solution)/shard_map/slice | solution.py:51
  66.9 3.5 %fusion.31 = bf16[1,256,512]{2,1,0:T(8,128)(2,1)S(1)} fusion(f32[1,256,512]{2,1,0:T(8,128)} %copy.46, f32[512]{0:T(512)S(1)} %fusion.36, f32[256]{0:T(256)S(1)} %add_convert_fusion, pred[512]{0:T(512)(128)(4,1)S(1)} %fusion.33), kind=kLoop, calls=%fused_computation.52 | loop fusion | flops 524288 | bytes 790016 | tf_op jit(solution)/shard_map/convert_element_type | solution.py:64
  71.1 7.3 %all_gather.9 = bf16[1,256,1024]{2,1,0:T(8,128)(2,1)S(1)} all-gather(bf16[1,256,512]{2,1,0:T(8,128)(2,1)S(1)} %fusion.31), channel_id=1, replica_groups=mesh['groups'=2,'seq'=4,'mp'=2,'section'=2] {'mp'}, dimensions={2}, use_global_device_ids=true | all-gather | bytes 786432 | tf_op jit(solution)/shard_map/all_gather | solution.py:65
  82.1 28.3 %all-gather.5.cloned.1.call-done = bf16[1,1024,1,512]{3,1,2,0:T(8,128)(2,1)} async-done(((bf16[1,256,1,512]{3,1,2,0:T(8,128)(2,1)}), bf16[1,1024,1,512]{3,1,2,0:T(8,128)(2,1)}) %all-gather.5.cloned.1.call-update) | async-done | bytes 1048592 | tf_op jit(solution)/shard_map/all_gather | solution.py:71
  110.4 2.3 copy.53
  112.6 16.1 %while.37 = (s32[]{:T(128)}, f32[1,8,256]{2,1,0:T(8,128)S(1)}, f32[1,8,256]{2,1,0:T(8,128)S(1)}, s32[2]{0:T(128)S(1)}, bf16[1,1024,512]{1,2,0:T(8,128)(2,1)}, /*...) while((s32[]{:T(128)}, f32[1,8,256]{2,1,0:T(8,128)S(1)}, ...), condition=%wide.region_4.5_spmd.clone, body=%wide.region_1.4_spmd.clone.sunk | while | flops 139470848 | bytes 10330286 | solution.py:101
  115.0 2.7 bitcast_reduce_fusion.2
  117.7 3.0 %fusion.86 = f32[8,256]{1,0:T(8,128)S(1)} fusion(f32[8,512,256]{2,1,0:T(8,128)} %get-tuple-element.514, f32[8,256]{1,0:T(8,128)S(1)} %bitcast.239), kind=kLoop, calls=%fused_computation.3.clone.1 | loop fusion | flops 3143680 | bytes 4210688 | tf_op jit(solution)/shard_map/while/body/eval_jaxpr/reduce_sum | solution.py:95
  123.1 2.7 bitcast_reduce_fusion.2
  125.8 2.9 %fusion.86 = f32[8,256]{1,0:T(8,128)S(1)} fusion(f32[8,512,256]{2,1,0:T(8,128)} %get-tuple-element.514, f32[8,256]{1,0:T(8,128)S(1)} %bitcast.239), kind=kLoop, calls=%fused_computation.3.clone.1 | loop fusion | flops 3143680 | bytes 4210688 | tf_op jit(solution)/shard_map/while/body/eval_jaxpr/reduce_sum | solution.py:95
  128.7 10.6 %all-gather.7.cloned.1.call-done = bf16[1,1024,1,512]{3,1,2,0:T(8,128)(2,1)} async-done(((bf16[1,256,1,512]{3,1,2,0:T(8,128)(2,1)}), bf16[1,1024,1,512]{3,1,2,0:T(8,128)(2,1)}) %all-gather.7.cloned.1.call-update) | async-done | bytes 1048592 | tf_op jit(solution)/shard_map/all_gather | solution.py:72
  139.4 2.3 copy.54
  141.7 13.9 %while.38 = (s32[]{:T(128)}, f32[1,256,8,64]{1,3,2,0:T(8,128)}, s32[2]{0:T(128)S(1)}, bf16[1,1024,512]{1,2,0:T(8,128)(2,1)}, bf16[1,1024,512]{1,2,0:T(8,128)(2,1...) while((s32[]{:T(128)}, f32[1,256,8,64]{1,3,2,0:T(8,128)}, ...), condition=%wide.region_6.7_spmd.clone, body=%wide.region_5.6_spmd.clone.sunk | while | flops 272891904 | bytes 4473021 | solution.py:116
  142.9 2.3 constant_dynamic-slice_fusion.9
  145.2 3.4 %fusion.90 = f32[1,256,8,64]{1,3,2,0:T(8,128)} fusion(bf16[512,8,64]{0,2,1:T(8,128)(2,1)} %bitcast.236, bf16[512,8,64]{0,2,1:T(8,128)(2,1)} %bitcast.235, f32[8,256]{1,0:T(8,128)S(1)} %bitcast.249, f32[8,256]{1,0:T(8,128)S(1)} %bitcast.245, f32[1,256,8,64]{1,3,2,0:T(8,128)} %get-tuple-element.581, ...), kind=kOutput, calls=%fused_computation.13.clone.1 | convolution fusion | flops 272891904 | bytes 2375681 | tf_op jit(solution)/shard_map/while/body/eval_jaxpr/chfk,ckhe->cfhe/dot_general | solution.py:111
  149.8 2.3 constant_dynamic-slice_fusion.9
  152.0 3.6 %fusion.90 = f32[1,256,8,64]{1,3,2,0:T(8,128)} fusion(bf16[512,8,64]{0,2,1:T(8,128)(2,1)} %bitcast.236, bf16[512,8,64]{0,2,1:T(8,128)(2,1)} %bitcast.235, f32[8,256]{1,0:T(8,128)S(1)} %bitcast.249, f32[8,256]{1,0:T(8,128)S(1)} %bitcast.245, f32[1,256,8,64]{1,3,2,0:T(8,128)} %get-tuple-element.581, ...), kind=kOutput, calls=%fused_computation.13.clone.1 | convolution fusion | flops 272891904 | bytes 2375681 | tf_op jit(solution)/shard_map/while/body/eval_jaxpr/chfk,ckhe->cfhe/dot_general | solution.py:111
  160.3 31.9 %psum.7 = f32[2]{0:T(128)S(1)} all-reduce(f32[2]{0:T(128)S(1)} %compare_select_fusion.2), channel_id=1, replica_groups=mesh['groups'=2,'seq'=4,'mp'=2,'section'=2] {'seq','mp','section'}, use_global_device_ids=true, to_apply=%region_8.9 | all-reduce | flops 2 | bytes 16 | tf_op jit(solution)/shard_map/psum | solution.py:128
  198.3 25.0 %while.39 = (s32[]{:T(128)}, f32[1,256,8,64]{1,3,2,0:T(8,128)}, bf16[2,512,1,1024]{1,3,2,0:T(8,128)(2,1)}, s32[2]{0:T(128)S(1)}, bf16[1,1024,512]{1,2,0:T(8,128)...) while((s32[]{:T(128)}, f32[1,256,8,64]{1,3,2,0:T(8,128)}, ...), condition=%wide.region_14.15_spmd.clone, body=%wide.region_13.14_spmd.clone.sunk | while | flops 681705472 | bytes 39346984 | solution.py:170
  207.7 3.0 %fusion.101 = f32[1,256,8,64]{1,3,2,0:T(8,128)} fusion(bf16[512,8,64]{0,2,1:T(8,128)(2,1)} %bitcast.227, bf16[8,512,256]{2,1,0:T(8,128)(2,1)} %copy-done.1, f32[1,256,8,64]{1,3,2,0:T(8,128)} %get-tuple-element.620, pred[]{:T(512)S(6)} %compare.19), kind=kOutput, calls=%fused_computation.27.clone.1 | convolution fusion | flops 134610944 | bytes 3670017 | tf_op jit(solution)/shard_map/while/body/eval_jaxpr/chfk,ckhe->cfhe/dot_general | solution.py:151
  220.2 3.1 %fusion.101 = f32[1,256,8,64]{1,3,2,0:T(8,128)} fusion(bf16[512,8,64]{0,2,1:T(8,128)(2,1)} %bitcast.227, bf16[8,512,256]{2,1,0:T(8,128)(2,1)} %copy-done.1, f32[1,256,8,64]{1,3,2,0:T(8,128)} %get-tuple-element.620, pred[]{:T(512)S(6)} %compare.19), kind=kOutput, calls=%fused_computation.27.clone.1 | convolution fusion | flops 134610944 | bytes 3670017 | tf_op jit(solution)/shard_map/while/body/eval_jaxpr/chfk,ckhe->cfhe/dot_general | solution.py:151
  223.3 3.3 %copy.58 = bf16[2,1,128,8,512]{4,3,0,2,1:T(8,128)(2,1)} copy(bf16[2,1,128,8,512]{4,3,2,1,0:T(8,128)(2,1)} %bitcast.70) | data formatting | bytes 4194304 | tf_op jit(solution)/shard_map/reshape | solution.py:171
  227.7 40.2 %reduce-scatter.2.cloned.1.call-done = bf16[256,1,1024]{0,2,1:T(8,128)(2,1)} async-done(((bf16[1024,1,1024]{0,2,1:T(8,128)(2,1)}), bf16[256,1,1024]{0,2,1:T(8,128)(2,1)}) %reduce-scatter.2.cloned.1.call-update) | async-done | bytes 524304 | tf_op jit(solution)/shard_map/reduce_scatter | solution.py:172
  269.9 2.3 copy.56
  (100 shorter events, 49.0 us)
Async XLA Ops:
  7.2 71.4 %copy-start = (bf16[1024,3,512]{2,0,1:T(8,128)(2,1)S(1)}, bf16[1024,3,512]{2,0,1:T(8,128)(2,1)}, u32[]{:S(2)}) copy-start(bf16[1024,3,512]{2,0,1:T(8,128)(2,1)} %param.17) | copy-start | bytes 9437188
  7.2 103.2 %all-gather.5.cloned.1.call-start = ((), (), s32[]{:S(2)}) async-start(), calls=%async_computation.2 | async-start | bytes 1310720 | tf_op jit(solution)/shard_map/all_gather | solution.py:71
  15.8 1.0 copy-start.5
  17.0 9.6 %collective-permute-start = (bf16[1,256,4]{2,1,0:T(8,128)(2,1)S(1)}, bf16[1,256,4]{2,1,0:T(8,128)(2,1)S(1)}, u32[]{:S(2)}, u32[]{:S(2)}) collective-permute-start(bf16[1,256,4]{2,1,0:T(8,128)(2,1)S(1)} %get-tuple-element.365), channel_id=1, source_target_pairs={{0,4},{4,8},{8,12},{1,5},{5,9},{9,13},{2,6},{6,10},{10,14},{3,7},{... | collective-permute-start | bytes 6152 | tf_op jit(solution)/shard_map/ppermute | solution.py:18
  21.9 6.2 %collective-permute-start.1 = (bf16[1,256,4]{2,1,0:T(8,128)(2,1)S(1)}, bf16[1,256,4]{2,1,0:T(8,128)(2,1)S(1)}, u32[]{:S(2)}, u32[]{:S(2)}) collective-permute-start(bf16[1,256,4]{2,1,0:T(8,128)(2,1)S(1)} %get-tuple-element.364), channel_id=1, source_target_pairs={{4,0},{8,4},{12,8},{5,1},{9,5},{13,9},{6,2},{10,6},{14,10},{7,3},{... | collective-permute-start | bytes 6152 | tf_op jit(solution)/shard_map/ppermute | solution.py:21
  61.7 1.9 copy-start.6
  70.4 0.7 copy-start.7
  78.6 2.1 copy-start.9
  80.6 58.8 %all-gather.7.cloned.1.call-start = ((), (), s32[]{:S(2)}) async-start(), calls=%async_computation.3 | async-start | bytes 1310720 | tf_op jit(solution)/shard_map/all_gather | solution.py:72
  81.8 186.0 %reduce-scatter.2.cloned.1.call-start = ((), (), s32[]{:S(2)}) async-start(), calls=%async_computation.1 | async-start | bytes 2621440 | tf_op jit(solution)/shard_map/reduce_scatter | solution.py:172
  141.7 16.1 %copy-start.8 = (f32[512]{0:T(512)S(1)}, f32[512]{0:T(512)}, u32[]{:S(2)}) copy-start(f32[512]{0:T(512)} %param.18) | copy-start | bytes 6148
  141.7 50.6 %copy-start.10 = (s32[4]{0:T(128)S(1)}, s32[4]{0:T(128)}, u32[]{:S(2)}) copy-start(s32[4]{0:T(128)} %param.21) | copy-start | bytes 52
  155.6 38.7 %copy-start.3 = (bf16[1,256,8,64]{1,3,2,0:T(8,128)(2,1)}, bf16[1,256,8,64]{1,3,2,0:T(8,128)(2,1)S(1)}, u32[]{:S(2)}) copy-start(bf16[1,256,8,64]{1,3,2,0:T(8,128)(2,1)S(1)} %get-tuple-element.656) | copy-start | bytes 786436
  192.2 6.1 %copy-start.11 = (f32[2]{0:T(128)}, f32[2]{0:T(128)S(1)}, u32[]{:S(2)}) copy-start(f32[2]{0:T(128)S(1)} %psum.7) | copy-start | bytes 28
  200.8 2.2 copy-start.2
  203.0 2.1 copy-start.4
  203.8 1.3 copy-start.1
  213.3 2.2 copy-start.2
  215.5 2.1 copy-start.4
  216.3 1.3 copy-start.1
Sparse Core Ops, SparseCore 0:
  80.7 29.6 all-gather.4
  111.9 27.4 all-gather.6
  226.7 41.0 reduce-scatter.1
where the time goes:
time: 280 us; the launch traced here: 279 us
  waiting for transfers between devices  80.7 us (29%)
  local copies, waits for them, and re-layouts  71.9 us (26%)
  blocking collectives  39.2 us (14%)
  other arithmetic  31.1 us (11%)
  matrix products  29.7 us (11%)
  between operations  15.3 us (5%)
  starting transfers between devices  6.74 us (2%)
  loops' own time  4.08 us (1%)
    reduce_scatter x1, waiting for transfers between devices, local(): lax.psum_scatter(stacked.astype(f32).astype(jnp.bfloat16), 'seq', scatter...  40.2 us
    psum x1, blocking collectives, local(): lax.psum(jnp.sum(owner * partial_rewards[:, None], axis=0), ('seq', 'mp',...  31.9 us
    all_gather x1, waiting for transfers between devices, local(): lax.all_gather(qkv[:, :, 1], 'seq', axis=1, tiled=True)  28.3 us
    slice x2, local copies, waits for them, and re-layouts, local(): blocks[:, :, :-1]  14.2 us
    all_gather x1, waiting for transfers between devices, local(): lax.all_gather(qkv[:, :, 2], 'seq', axis=1, tiled=True)  10.6 us
    dot_general x4, matrix products, scores_for(): jnp.einsum('cfhe,ckhe->chfk', query4, key_slice(keys, start, size), prefe...  9.74 us
    dynamic_slice x6, local copies, waits for them, and re-layouts, key_slice(): lax.dynamic_slice_in_dim(source, start, size, 1)  9.22 us
    unnamed x21, local copies, waits for them, and re-layouts  8.64 us
  transfers between devices with their start and end apart: 5, of which 4 were waited for; matrix products, arithmetic and copies ran while one was open for 8% of the time, Pallas kernels for 0%

commit v1 on v0

--- a/solution.py
+++ b/solution.py
@@ -125,7 +125,9 @@
         == (section_id * cand + jnp.arange(cand, dtype=jnp.int32))[:, None]
     ).astype(f32)
     partial_rewards = jnp.sum(attended * gate * readout, axis=(1, 2)) / math.sqrt(total)
-    rewards = lax.psum(jnp.sum(owner * partial_rewards[:, None], axis=0), ("seq", "mp", "section"))
+    rewards = lax.psum(
+        lax.psum(jnp.sum(owner * partial_rewards[:, None], axis=0), ("mp", "section")), "seq"
+    )
     chosen = (pairs[:, :, None] == jnp.arange(all_cands, dtype=jnp.int32)[None, None, :]).astype(
         f32
     )

time: 280 us -> 266 us (0.950)
  blocking collectives: 39.2 us -> 24.4 us
    psum x1 -> x2, blocking collectives: 31.9 us -> 17.1 us  [the longest x1 10.7 us: local(): lax.psum(lax.psum(jnp.sum(owner * partial_rewards[:, None], axis=0), ('mp...]
where the time goes in v1:
time: 266 us; the launch traced here: 264 us
  waiting for transfers between devices  81 us (30%)
  local copies, waits for them, and re-layouts  72 us (27%)
  other arithmetic  31.2 us (12%)
  matrix products  29.7 us (11%)
  blocking collectives  24.4 us (9%)
  between operations  15.3 us (6%)
  starting transfers between devices  6.74 us (3%)
  loops' own time  4.19 us (2%)
    reduce_scatter x1, waiting for transfers between devices, local(): lax.psum_scatter(stacked.astype(f32).astype(jnp.bfloat16), 'seq', scatter...  40.2 us
    all_gather x1, waiting for transfers between devices, local(): lax.all_gather(qkv[:, :, 1], 'seq', axis=1, tiled=True)  28.3 us
    slice x2, local copies, waits for them, and re-layouts, local(): blocks[:, :, :-1]  14.2 us
    all_gather x1, waiting for transfers between devices, local(): lax.all_gather(qkv[:, :, 2], 'seq', axis=1, tiled=True)  11 us
    psum x1, blocking collectives, local(): lax.psum(lax.psum(jnp.sum(owner * partial_rewards[:, None], axis=0), ('mp...  10.7 us
    dot_general x4, matrix products, scores_for(): jnp.einsum('cfhe,ckhe->chfk', query4, key_slice(keys, start, size), prefe...  9.71 us
    dynamic_slice x6, local copies, waits for them, and re-layouts, key_slice(): lax.dynamic_slice_in_dim(source, start, size, 1)  9.18 us
    unnamed x21, local copies, waits for them, and re-layouts  8.66 us
  transfers between devices with their start and end apart: 5, of which 4 were waited for; matrix products, arithmetic and copies ran while one was open for 8% of the time, Pallas kernels for 0%

profile of v1, /device:TPU:0, one launch (start us, length us, event | category | flops | bytes accessed | tf_op | source)
XLA Modules:
  0.0 264.4 jit_solution(8172814715798387354)
XLA Ops:
  7.2 8.6 %fusion.25 = bf16[1,256,2048]{2,1,0:T(8,128)(2,1)S(1)} fusion(bf16[1,256,2048]{2,1,0:T(8,128)(2,1)} %param.14, f32[256]{0:T(256)} %param.15), kind=kLoop, calls=%fused_computation.40 | loop fusion | flops 3145728 | bytes 2098176 | tf_op jit(solution)/shard_map/convert_element_type | solution.py:46
  17.0 4.9 %collective-permute-start = (bf16[1,256,4]{2,1,0:T(8,128)(2,1)S(1)}, bf16[1,256,4]{2,1,0:T(8,128)(2,1)S(1)}, u32[]{:S(2)}, u32[]{:S(2)}) collective-permute-start(bf16[1,256,4]{2,1,0:T(8,128)(2,1)S(1)} %get-tuple-element.365), channel_id=1, source_target_pairs={{0,4},{4,8},{8,12},{1,5},{5,9},{9,13},{2,6},{6,10},{10,14},{3,7},{... | collective-permute-start | bytes 6152 | tf_op jit(solution)/shard_map/ppermute | solution.py:18
  24.1 2.4 reshape.438
  28.1 3.5 %concatenate.32 = bf16[1,256,2056]{2,1,0:T(8,128)(2,1)} concatenate(bf16[1,256,4]{2,1,0:T(8,128)(2,1)S(1)} %collective-permute-done, bf16[1,256,2048]{2,1,0:T(8,128)(2,1)} %copy-done.5, bf16[1,256,4]{2,1,0:T(8,128)(2,1)S(1)} %collective-permute-done.1), dimensions={2} | concatenate | bytes 2105344 | tf_op jit(solution)/shard_map/concatenate | solution.py:22
  31.5 2.3 copy.41
  33.9 5.8 %reshape.436 = bf16[1,8,32,257,8]{2,1,4,3,0:T(8,128)(2,1)} reshape(bf16[1,256,2056]{1,2,0:T(8,128)(2,1)} %copy.41) | data formatting | bytes 2105344 | tf_op jit(solution)/shard_map/reshape | solution.py:48
  39.7 6.5 %fusion.53 = (bf16[1,8,256,32,8]{3,1,4,2,0:T(8,128)(2,1)}, bf16[1,8,256,32,8]{3,1,4,2,0:T(8,128)(2,1)}) fusion(bf16[1,8,257,32,8]{3,1,4,2,0:T(8,128)(2,1)} %bitcast.233), kind=kLoop, calls=%fused_computation.102 | loop fusion | bytes 4194304 | tf_op jit(solution)/shard_map/slice | solution.py:51
  46.2 7.7 %copy.42 = bf16[1,8,256,32,8]{2,4,3,1,0:T(8,128)(2,1)} copy(bf16[1,8,256,32,8]{3,1,4,2,0:T(8,128)(2,1)} %get-tuple-element.362) | data formatting | bytes 2097152 | tf_op jit(solution)/shard_map/slice | solution.py:51
  53.9 7.8 %copy.43 = bf16[1,8,256,32,8]{2,4,3,1,0:T(8,128)(2,1)} copy(bf16[1,8,256,32,8]{3,1,4,2,0:T(8,128)(2,1)} %get-tuple-element.363) | data formatting | bytes 2097152 | tf_op jit(solution)/shard_map/slice | solution.py:51
  66.9 3.5 %fusion.31 = bf16[1,256,512]{2,1,0:T(8,128)(2,1)S(1)} fusion(f32[1,256,512]{2,1,0:T(8,128)} %copy.46, f32[512]{0:T(512)S(1)} %fusion.36, f32[256]{0:T(256)S(1)} %add_convert_fusion, pred[512]{0:T(512)(128)(4,1)S(1)} %fusion.33), kind=kLoop, calls=%fused_computation.52 | loop fusion | flops 524288 | bytes 790016 | tf_op jit(solution)/shard_map/convert_element_type | solution.py:64
  71.1 7.3 %all_gather.9 = bf16[1,256,1024]{2,1,0:T(8,128)(2,1)S(1)} all-gather(bf16[1,256,512]{2,1,0:T(8,128)(2,1)S(1)} %fusion.31), channel_id=1, replica_groups=mesh['groups'=2,'seq'=4,'mp'=2,'section'=2] {'mp'}, dimensions={2}, use_global_device_ids=true | all-gather | bytes 786432 | tf_op jit(solution)/shard_map/all_gather | solution.py:65
  82.0 28.3 %all-gather.5.cloned.1.call-done = bf16[1,1024,1,512]{3,1,2,0:T(8,128)(2,1)} async-done(((bf16[1,256,1,512]{3,1,2,0:T(8,128)(2,1)}), bf16[1,1024,1,512]{3,1,2,0:T(8,128)(2,1)}) %all-gather.5.cloned.1.call-update) | async-done | bytes 1048592 | tf_op jit(solution)/shard_map/all_gather | solution.py:71
  110.3 2.3 copy.53
  112.6 16.3 %while.37 = (s32[]{:T(128)}, f32[1,8,256]{2,1,0:T(8,128)S(1)}, f32[1,8,256]{2,1,0:T(8,128)S(1)}, s32[2]{0:T(128)S(1)}, bf16[1,1024,512]{1,2,0:T(8,128)(2,1)}, /*...) while((s32[]{:T(128)}, f32[1,8,256]{2,1,0:T(8,128)S(1)}, ...), condition=%wide.region_4.5_spmd.clone, body=%wide.region_1.4_spmd.clone.sunk | while | flops 139470848 | bytes 10330286 | solution.py:101
  115.0 2.7 %bitcast_reduce_fusion.2 = (f32[8,256]{1,0:T(8,128)S(1)}, f32[8,512,256]{2,1,0:T(8,128)}) fusion(bf16[512,8,64]{0,2,1:T(8,128)(2,1)S(1)} %bitcast.228, bf16[1,256,8,64]{1,3,2,0:T(8,128)(2,1)S(1)} %get-tuple-element.563), kind=kOutput, calls=%fused_computation.1.clone.1 | convolution fusion | flops 136312832 | bytes 4988928 | tf_op jit(solution)/shard_map/while/body/eval_jaxpr/cfhe,ckhe->chfk/dot_general | solution.py:85
  117.7 3.0 %fusion.86 = f32[8,256]{1,0:T(8,128)S(1)} fusion(f32[8,512,256]{2,1,0:T(8,128)} %get-tuple-element.514, f32[8,256]{1,0:T(8,128)S(1)} %bitcast.239), kind=kLoop, calls=%fused_computation.3.clone.1 | loop fusion | flops 3143680 | bytes 4210688 | tf_op jit(solution)/shard_map/while/body/eval_jaxpr/reduce_sum | solution.py:95
  123.3 2.7 %bitcast_reduce_fusion.2 = (f32[8,256]{1,0:T(8,128)S(1)}, f32[8,512,256]{2,1,0:T(8,128)}) fusion(bf16[512,8,64]{0,2,1:T(8,128)(2,1)S(1)} %bitcast.228, bf16[1,256,8,64]{1,3,2,0:T(8,128)(2,1)S(1)} %get-tuple-element.563), kind=kOutput, calls=%fused_computation.1.clone.1 | convolution fusion | flops 136312832 | bytes 4988928 | tf_op jit(solution)/shard_map/while/body/eval_jaxpr/cfhe,ckhe->chfk/dot_general | solution.py:85
  126.0 2.9 %fusion.86 = f32[8,256]{1,0:T(8,128)S(1)} fusion(f32[8,512,256]{2,1,0:T(8,128)} %get-tuple-element.514, f32[8,256]{1,0:T(8,128)S(1)} %bitcast.239), kind=kLoop, calls=%fused_computation.3.clone.1 | loop fusion | flops 3143680 | bytes 4210688 | tf_op jit(solution)/shard_map/while/body/eval_jaxpr/reduce_sum | solution.py:95
  128.9 11.0 %all-gather.7.cloned.1.call-done = bf16[1,1024,1,512]{3,1,2,0:T(8,128)(2,1)} async-done(((bf16[1,256,1,512]{3,1,2,0:T(8,128)(2,1)}), bf16[1,1024,1,512]{3,1,2,0:T(8,128)(2,1)}) %all-gather.7.cloned.1.call-update) | async-done | bytes 1048592 | tf_op jit(solution)/shard_map/all_gather | solution.py:72
  139.9 2.3 copy.54
  142.2 13.9 %while.38 = (s32[]{:T(128)}, f32[1,256,8,64]{1,3,2,0:T(8,128)}, s32[2]{0:T(128)S(1)}, bf16[1,1024,512]{1,2,0:T(8,128)(2,1)}, bf16[1,1024,512]{1,2,0:T(8,128)(2,1...) while((s32[]{:T(128)}, f32[1,256,8,64]{1,3,2,0:T(8,128)}, ...), condition=%wide.region_6.7_spmd.clone, body=%wide.region_5.6_spmd.clone.sunk | while | flops 272891904 | bytes 4473021 | solution.py:116
  143.4 2.2 constant_dynamic-slice_fusion.9
  145.7 3.4 %fusion.90 = f32[1,256,8,64]{1,3,2,0:T(8,128)} fusion(bf16[512,8,64]{0,2,1:T(8,128)(2,1)} %bitcast.236, bf16[512,8,64]{0,2,1:T(8,128)(2,1)} %bitcast.235, f32[8,256]{1,0:T(8,128)S(1)} %bitcast.249, f32[8,256]{1,0:T(8,128)S(1)} %bitcast.245, f32[1,256,8,64]{1,3,2,0:T(8,128)} %get-tuple-element.581, ...), kind=kOutput, calls=%fused_computation.13.clone.1 | convolution fusion | flops 272891904 | bytes 2375681 | tf_op jit(solution)/shard_map/while/body/eval_jaxpr/chfk,ckhe->cfhe/dot_general | solution.py:111
  152.5 3.5 %fusion.90 = f32[1,256,8,64]{1,3,2,0:T(8,128)} fusion(bf16[512,8,64]{0,2,1:T(8,128)(2,1)} %bitcast.236, bf16[512,8,64]{0,2,1:T(8,128)(2,1)} %bitcast.235, f32[8,256]{1,0:T(8,128)S(1)} %bitcast.249, f32[8,256]{1,0:T(8,128)S(1)} %bitcast.245, f32[1,256,8,64]{1,3,2,0:T(8,128)} %get-tuple-element.581, ...), kind=kOutput, calls=%fused_computation.13.clone.1 | convolution fusion | flops 272891904 | bytes 2375681 | tf_op jit(solution)/shard_map/while/body/eval_jaxpr/chfk,ckhe->cfhe/dot_general | solution.py:111
  160.8 6.4 %psum.14 = f32[2]{0:T(128)S(1)} all-reduce(f32[2]{0:T(128)S(1)} %compare_select_fusion.2), channel_id=1, replica_groups=mesh['groups'=2,'seq'=4,'mp'=2,'section'=2] {'mp','section'}, use_global_device_ids=true, to_apply=%region_8.9 | all-reduce | flops 2 | bytes 16 | tf_op jit(solution)/shard_map/psum | solution.py:129
  167.2 10.7 %psum.15 = f32[2]{0:T(128)S(1)} all-reduce(f32[2]{0:T(128)S(1)} %psum.14), channel_id=1, replica_groups=mesh['groups'=2,'seq'=4,'mp'=2,'section'=2] {'seq'}, use_global_device_ids=true, to_apply=%region_9.10 | all-reduce | flops 2 | bytes 16 | tf_op jit(solution)/shard_map/psum | solution.py:128
  184.0 25.0 %while.39 = (s32[]{:T(128)}, f32[1,256,8,64]{1,3,2,0:T(8,128)}, bf16[2,512,1,1024]{1,3,2,0:T(8,128)(2,1)}, s32[2]{0:T(128)S(1)}, bf16[1,1024,512]{1,2,0:T(8,128)...) while((s32[]{:T(128)}, f32[1,256,8,64]{1,3,2,0:T(8,128)}, ...), condition=%wide.region_15.16_spmd.clone, body=%wide.region_14.15_spmd.clone.sunk | while | flops 681705472 | bytes 39346984 | solution.py:172
  193.4 3.0 %fusion.101 = f32[1,256,8,64]{1,3,2,0:T(8,128)} fusion(bf16[512,8,64]{0,2,1:T(8,128)(2,1)} %bitcast.227, bf16[8,512,256]{2,1,0:T(8,128)(2,1)} %copy-done.1, f32[1,256,8,64]{1,3,2,0:T(8,128)} %get-tuple-element.620, pred[]{:T(512)S(6)} %compare.19), kind=kOutput, calls=%fused_computation.27.clone.1 | convolution fusion | flops 134610944 | bytes 3670017 | tf_op jit(solution)/shard_map/while/body/eval_jaxpr/chfk,ckhe->cfhe/dot_general | solution.py:153
  205.9 3.1 %fusion.101 = f32[1,256,8,64]{1,3,2,0:T(8,128)} fusion(bf16[512,8,64]{0,2,1:T(8,128)(2,1)} %bitcast.227, bf16[8,512,256]{2,1,0:T(8,128)(2,1)} %copy-done.1, f32[1,256,8,64]{1,3,2,0:T(8,128)} %get-tuple-element.620, pred[]{:T(512)S(6)} %compare.19), kind=kOutput, calls=%fused_computation.27.clone.1 | convolution fusion | flops 134610944 | bytes 3670017 | tf_op jit(solution)/shard_map/while/body/eval_jaxpr/chfk,ckhe->cfhe/dot_general | solution.py:153
  209.0 3.3 %copy.58 = bf16[2,1,128,8,512]{4,3,0,2,1:T(8,128)(2,1)} copy(bf16[2,1,128,8,512]{4,3,2,1,0:T(8,128)(2,1)} %bitcast.70) | data formatting | bytes 4194304 | tf_op jit(solution)/shard_map/reshape | solution.py:173
  213.4 40.2 %reduce-scatter.2.cloned.1.call-done = bf16[256,1,1024]{0,2,1:T(8,128)(2,1)} async-done(((bf16[1024,1,1024]{0,2,1:T(8,128)(2,1)}), bf16[256,1,1024]{0,2,1:T(8,128)(2,1)}) %reduce-scatter.2.cloned.1.call-update) | async-done | bytes 524304 | tf_op jit(solution)/shard_map/reduce_scatter | solution.py:174
  255.6 2.3 copy.56
  (101 shorter events, 51.3 us)
Async XLA Ops:
  7.2 71.4 %copy-start = (bf16[1024,3,512]{2,0,1:T(8,128)(2,1)S(1)}, bf16[1024,3,512]{2,0,1:T(8,128)(2,1)}, u32[]{:S(2)}) copy-start(bf16[1024,3,512]{2,0,1:T(8,128)(2,1)} %param.17) | copy-start | bytes 9437188
  7.2 103.1 %all-gather.5.cloned.1.call-start = ((), (), s32[]{:S(2)}) async-start(), calls=%async_computation.2 | async-start | bytes 1310720 | tf_op jit(solution)/shard_map/all_gather | solution.py:71
  15.8 1.0 copy-start.5
  17.0 9.6 %collective-permute-start = (bf16[1,256,4]{2,1,0:T(8,128)(2,1)S(1)}, bf16[1,256,4]{2,1,0:T(8,128)(2,1)S(1)}, u32[]{:S(2)}, u32[]{:S(2)}) collective-permute-start(bf16[1,256,4]{2,1,0:T(8,128)(2,1)S(1)} %get-tuple-element.365), channel_id=1, source_target_pairs={{0,4},{4,8},{8,12},{1,5},{5,9},{9,13},{2,6},{6,10},{10,14},{3,7},{... | collective-permute-start | bytes 6152 | tf_op jit(solution)/shard_map/ppermute | solution.py:18
  21.9 6.2 %collective-permute-start.1 = (bf16[1,256,4]{2,1,0:T(8,128)(2,1)S(1)}, bf16[1,256,4]{2,1,0:T(8,128)(2,1)S(1)}, u32[]{:S(2)}, u32[]{:S(2)}) collective-permute-start(bf16[1,256,4]{2,1,0:T(8,128)(2,1)S(1)} %get-tuple-element.364), channel_id=1, source_target_pairs={{4,0},{8,4},{12,8},{5,1},{9,5},{13,9},{6,2},{10,6},{14,10},{7,3},{... | collective-permute-start | bytes 6152 | tf_op jit(solution)/shard_map/ppermute | solution.py:21
  61.7 1.9 copy-start.6
  70.4 0.7 copy-start.7
  78.6 2.0 copy-start.9
  80.5 59.4 %all-gather.7.cloned.1.call-start = ((), (), s32[]{:S(2)}) async-start(), calls=%async_computation.3 | async-start | bytes 1310720 | tf_op jit(solution)/shard_map/all_gather | solution.py:72
  81.8 171.8 %reduce-scatter.2.cloned.1.call-start = ((), (), s32[]{:S(2)}) async-start(), calls=%async_computation.1 | async-start | bytes 2621440 | tf_op jit(solution)/shard_map/reduce_scatter | solution.py:174
  142.2 16.0 %copy-start.8 = (f32[512]{0:T(512)S(1)}, f32[512]{0:T(512)}, u32[]{:S(2)}) copy-start(f32[512]{0:T(512)} %param.18) | copy-start | bytes 6148
  142.2 35.7 %copy-start.10 = (s32[4]{0:T(128)S(1)}, s32[4]{0:T(128)}, u32[]{:S(2)}) copy-start(s32[4]{0:T(128)} %param.21) | copy-start | bytes 52
  156.1 23.9 %copy-start.3 = (bf16[1,256,8,64]{1,3,2,0:T(8,128)(2,1)}, bf16[1,256,8,64]{1,3,2,0:T(8,128)(2,1)S(1)}, u32[]{:S(2)}) copy-start(bf16[1,256,8,64]{1,3,2,0:T(8,128)(2,1)S(1)} %get-tuple-element.656) | copy-start | bytes 786436
  177.8 6.1 %copy-start.11 = (f32[2]{0:T(128)}, f32[2]{0:T(128)S(1)}, u32[]{:S(2)}) copy-start(f32[2]{0:T(128)S(1)} %psum.15) | copy-start | bytes 28
  186.5 2.2 copy-start.2
  188.7 2.1 copy-start.4
  189.5 1.4 copy-start.1
  199.0 2.2 copy-start.2
  201.2 2.1 copy-start.4
  202.0 1.4 copy-start.1
Sparse Core Ops, SparseCore 0:
  80.7 29.5 all-gather.4
  112.4 27.4 all-gather.6
  212.4 41.0 reduce-scatter.1
